TPU v7x, 32 devices: a whole 2x2x4 slice. The times are simulated.
32 devices in a mesh: row: 4 (over y, x), col: 8 (over z, core).
Axes of the slice: x: 2, y: 2, z: 4, core: 2. Of those that a mesh axis runs over, the one named last changes fastest.
Arguments:
- wavefield: bfloat16 [2, 1, 8192, 8192], P(None, None, 'row', 'col'), as said below
- panel_order: int32 [16], replicated, may hold values from 0 to 15, each once
- filter_taps: float32 [11, 8192], P(None, 'col'), may hold values from -4 to 4
Outputs:
- primaries: bfloat16 [2, 1, 8192, 8192], P(None, None, 'row', 'col')
Inputs may be any that keep to these rules, and one draw needn't show every extreme that they name: Reciprocity: wavefield[c, f, s, r] = wavefield[c, f, r, s] for every part, frequency, shot and receiver.
All inputs are finite; a program needn't handle non-finite values.
Results may differ from a plain program's by a relative error of at most 0.00045.
Values may be sent and summed in bfloat16 or wider, within the bound.
A program may use at most 128 MiB of HBM per device.

v0:
```python
import math
import jax
import jax.numpy as jnp
from jax import lax
from jax.sharding import PartitionSpec as P

SIDE = 8192
PANEL = 512
STEPS = 3
TAPS = 11
FIRST_FREQUENCY = 8
NT = 1024


def spread(block, axis, holder):
    block = jnp.where(lax.axis_index(axis) == holder, block, jnp.zeros_like(block))
    return lax.psum(block, axis)


def frequency_spectrum(filter_taps, freq_count):
    lags = jnp.arange(TAPS, dtype=jnp.float32)
    omega = 2.0 * math.pi * (FIRST_FREQUENCY + jnp.arange(freq_count, dtype=jnp.float32)) / NT
    phase = omega[:, None] * lags[None, :]
    real_part = jnp.dot(jnp.cos(phase), filter_taps, precision=lax.Precision.HIGHEST)
    imag_part = -jnp.dot(jnp.sin(phase), filter_taps, precision=lax.Precision.HIGHEST)
    return (real_part, imag_part)


def local(wavefield, panel_order, filter_taps):
    freq_count = wavefield.shape[1]
    shot_block = wavefield.shape[2]
    recv_block = wavefield.shape[3]
    own_row_index = lax.axis_index("row")
    factor = 1.0 / math.sqrt(STEPS * PANEL)
    count = 2.0 * SIDE * SIDE
    local_data = jnp.sum(jnp.square(wavefield.astype(jnp.float32)), axis=(0, 2, 3))
    energy_data = lax.psum(local_data, ("row", "col"))
    totals = jnp.zeros((freq_count, shot_block, 2 * recv_block), jnp.float32)
    for panel_advance in range(STEPS):
        first_point = panel_order[panel_advance] * PANEL
        row_width = min(PANEL, shot_block)
        owner_turn = 0
        start = first_point + owner_turn * row_width
        piece = lax.dynamic_slice_in_dim(wavefield, start % shot_block, row_width, 2)
        row_pieces = spread(piece, "row", start // shot_block)
        col_pieces = []
        mirror_width = min(shot_block, recv_block)
        for owner_turn in range(max(1, shot_block // recv_block)):
            start = own_row_index * shot_block + owner_turn * mirror_width
            piece = row_pieces
            col_pieces.append(spread(piece, "col", start // recv_block))
        upper = jnp.swapaxes(jnp.concatenate(col_pieces, axis=3), 2, 3)
        left_factor = jnp.concatenate([upper[0], upper[1]], axis=2)
        right_factor = jnp.concatenate(
            [
                jnp.concatenate([row_pieces[0], row_pieces[1]], axis=2),
                jnp.concatenate([-row_pieces[1], row_pieces[0]], axis=2),
            ],
            axis=1,
        )
        totals = totals + jnp.einsum(
            "yga,yah->ygh", left_factor, right_factor, preferred_element_type=jnp.float32
        )
    mult_re = totals[:, :, :recv_block] * factor
    mult_im = totals[:, :, recv_block:] * factor
    local_mult = jnp.sum(mult_re * mult_re, axis=(1, 2)) + jnp.sum(mult_im * mult_im, axis=(1, 2))
    energy_mult = lax.psum(local_mult, ("row", "col"))
    gain = jnp.sqrt((energy_data / count + 1e-05) / (energy_mult / count + 1e-05))[:, None, None]
    spec_re, spectrum_imaginary = frequency_spectrum(filter_taps, freq_count)
    a_re = spec_re[:, None, :]
    a_im = spectrum_imaginary[:, None, :]
    sub_re = gain * (a_re * mult_re - a_im * mult_im)
    subtracted_imaginary = gain * (a_re * mult_im + a_im * mult_re)
    result = jnp.stack(
        [
            wavefield[0].astype(jnp.float32) - sub_re,
            wavefield[1].astype(jnp.float32) - subtracted_imaginary,
        ]
    )
    return result.astype(jnp.bfloat16)


def solution(mesh):
    in_specs = (P(None, None, "row", "col"), P(), P(None, "col"))
    out_specs = P(None, None, "row", "col")
    return jax.shard_map(local, mesh=mesh, in_specs=in_specs, out_specs=out_specs, check_vma=False)
```

profile of v0, /device:TPU:0, one launch (start us, length us, event | category | flops | bytes accessed | tf_op | source)
XLA Modules:
  0.0 574.6 jit_solution(4812918331580029134)
XLA Ops:
  6.5 1.4 fusion.46
  9.9 7.0 %dynamic-slice_select_fusion = (bf16[2,1,512,1024]{3,2,1,0:T(8,128)(2,1)}, bf16[2,1,512,1024]{3,2,1,0:T(8,128)(2,1)}, bf16[2,1,512,1024]{3,2,1,0:T(8,128)(2,1)}) fusion(bf16[2,1,2048,1024]{3,2,1,0:T(8,128)(2,1)} %param.3, s32[]{:T(128)S(6)} %select_n.113, pred[]{:T(512)S(6)} %eq.27, s32[]{:T(128)S(6)} %select_n.106, pred[]{:T(512)S(6)} %eq.26, ...), kind=kLoop, calls=%fused_computation.52 | loop fusion | flops 3145728 | bytes 12582927 | tf_op jit(solution)/shard_map/jit(_where)/select_n | solution.py:16
  16.9 0.2 all-reduce.6.cloned.1.call-start
  17.2 140.8 %all-reduce.8.cloned.1.call-done = (bf16[2,1,512,1024]{3,2,1,0:T(8,128)(2,1)}, bf16[2,1,512,1024]{3,2,1,0:T(8,128)(2,1)}, bf16[2,1,512,1024]{3,2,1,0:T(8,128)(2,1)}) async-done(((bf16[2,1,512,1024]{3,2,1,0:T(8,128)(2,1)}, bf16[2,1,512,1024]{3,2,1,0:T(8,128)(2,1)}, bf16[2,1,512,1024]{3,2,1,0:T(8,128)(2,1)}), (bf16[2,1,512,1024]{3,2,1,0:T(8,128)(2,1)}, bf16[2,1,512,1024]{3,2,1,0:T(8,128)(2,1)}, ...) | async-done | bytes 6291472 | tf_op jit(solution)/shard_map/psum | solution.py:17
  158.0 4.0 broadcast_select_fusion.5
  162.0 3.5 broadcast_select_fusion.3
  165.5 0.2 fusion.30
  165.7 0.2 fusion.32
  166.0 8.5 %multiply_reduce_fusion = f32[]{:T(128)} fusion(bf16[2,1,2048,1024]{3,2,1,0:T(8,128)(2,1)} %param.3), kind=kLoop, calls=%fused_computation.1 | loop fusion | flops 12582911 | bytes 8388612 | tf_op jit(solution)/shard_map/reduce_sum | solution.py:36
  174.4 0.1 fusion.45
  174.5 1.6 slice_bitcast_fusion.10
  176.1 0.7 copy-done.4
  176.8 1.6 fusion.43
  178.4 2.1 slice_bitcast_fusion.6
  180.5 239.8 %all-reduce.6.cloned.1.call-done = (bf16[2,1,512,1024]{3,2,1,0:T(8,128)(2,1)}, bf16[2,1,512,1024]{3,2,1,0:T(8,128)(2,1)}, bf16[2,1,512,1024]{3,2,1,0:T(8,128)(2,...) async-done(((bf16[2,1,512,1024]{3,2,1,0:T(8,128)(2,1)}, bf16[2,1,512,1024]{3,2,1,0:T(8,128)(2,1)}, ...) | async-done | bytes 12582928 | tf_op jit(solution)/shard_map/psum | solution.py:17
  420.4 2.7 maximum_bitcast_fusion
  423.1 0.3 slice_bitcast_fusion.5
  423.4 1.3 copy-done.8
  424.7 0.6 copy-done.9
  425.3 0.4 maximum_bitcast_fusion.5
  425.8 0.6 slice_bitcast_fusion.3
  426.4 1.0 copy-done.6
  427.4 0.6 copy-done.7
  428.0 0.4 maximum_bitcast_fusion.10
  428.4 0.6 slice_bitcast_fusion.1
  429.0 14.7 %fusion.13 = f32[2048,2048]{1,0:T(8,128)} fusion(bf16[1,2048,512]{1,2,0:T(8,128)(2,1)S(1)} %get-tuple-element.26, bf16[1,2048,512]{1,2,0:T(8,128)(2,1)S(1)} %get-tuple-element.25, bf16[1,512,1024]{2,1,0:T(8,128)(2,1)} %get-tuple-element.46, bf16[1,512,1024]{2,1,0:T(8,128)(2,1)} %get-tuple-element.49, bf16[1,512,1024]{2,1,0:T(8,128)(2,1)} %get-tuple-element.47), kind=kOutput, calls=%fused_computation.25 | convolution fusion | flops 8615100416 | bytes 24117248 | tf_op jit(solution)/shard_map/yga,yah->ygh/dot_general | solution.py:61
  443.8 25.3 %fusion.4 = f32[2048,2048]{1,0:T(8,128)} fusion(bf16[1,2048,512]{1,2,0:T(8,128)(2,1)S(1)} %get-tuple-element.28, bf16[1,2048,512]{1,2,0:T(8,128)(2,1)S(1)} %get-tuple-element.27, bf16[1,512,1024]{2,1,0:T(8,128)(2,1)S(1)} %copy-done.11, bf16[1,512,1024]{2,1,0:T(8,128)(2,1)S(1)} %copy-done.12, bf16[1,512,1024]{2,1,0:T(8,128)(2,1)S(1)} %copy-done.10), kind=kOutput, calls=%fused_computation.13 | convolution fusion | flops 8615100416 | bytes 24117248 | tf_op jit(solution)/shard_map/yga,yah->ygh/dot_general | solution.py:61
  469.1 29.0 %add_bitcast_fusion = f32[1,2048,2048]{2,1,0:T(8,128)} fusion(f32[2048,2048]{1,0:T(8,128)} %fusion.4, f32[2048,2048]{1,0:T(8,128)} %fusion.13, bf16[1,2048,512]{1,2,0:T(8,128)(2,1)S(1)} %get-tuple-element.24, bf16[1,2048,512]{1,2,0:T(8,128)(2,1)S(1)} %get-tuple-element.23, bf16[1,512,1024]{2,1,0:T(8,128)(2,1)S(1)} %copy-done.14, ...), kind=kOutput, calls=%fused_computation | convolution fusion | flops 8623489024 | bytes 57671680 | tf_op jit(solution)/shard_map/yga,yah->ygh/dot_general | solution.py:61
  498.1 7.5 %multiply_reduce_fusion.1 = (f32[]{:T(128)}, f32[]{:T(128)}) fusion(f32[1,2048,2048]{2,1,0:T(8,128)} %add_bitcast_fusion), kind=kLoop, calls=%fused_computation.7 | loop fusion | flops 12582910 | bytes 16777224 | tf_op jit(solution)/shard_map/reduce_sum | solution.py:66
  506.9 40.9 %all-reduce = (f32[1]{0:T(128)}, f32[1]{0:T(128)}) all-reduce(f32[1]{0:T(128)} %bitcast.1, f32[1]{0:T(128)} %bitcast.27), channel_id=1, replica_groups=mesh['row'=4,'col'=8] {'row','col'}, use_global_device_ids=true, to_apply=%region_1.0 | all-reduce | flops 2 | bytes 16 | tf_op jit(solution)/shard_map/psum | solution.py:37
  549.1 12.3 %fusion.2 = (bf16[1,1,2048,1024]{3,2,1,0:T(8,128)(2,1)S(1)}, bf16[1,1,2048,1024]{3,2,1,0:T(8,128)(2,1)}) fusion(f32[1,2048,2048]{2,1,0:T(8,128)} %add_bitcast_fusion, f32[1024]{0:T(1024)S(1)} %get-tuple-element.50, f32[1024]{0:T(1024)S(1)} %get-tuple-element.51, f32[]{:T(128)} %bitcast.28, bf16[2,1,2048,1024]{3,2,1,0:T(8,128)(2,1)} %param.3), kind=kLoop, calls=%fused_computation.9 | loop fusion | flops 29360128 | bytes 33562628 | tf_op jit(solution)/shard_map/stack | solution.py:74
  561.3 6.4 %pad_maximum_fusion = bf16[2,1,2048,1024]{3,2,1,0:T(8,128)(2,1)} fusion(bf16[1,1,2048,1024]{3,2,1,0:T(8,128)(2,1)} %get-tuple-element.19, bf16[1,1,2048,1024]{3,2,1,0:T(8,128)(2,1)S(1)} %get-tuple-element.18), kind=kLoop, calls=%fused_computation.2 | loop fusion | flops 4194304 | bytes 16777216 | tf_op jit(solution)/shard_map/stack | solution.py:74
  (29 shorter events, 0.1 us)
Async XLA Ops:
  6.5 159.0 %copy-start = (f32[11,1024]{1,0:T(8,128)S(1)}, f32[11,1024]{1,0:T(8,128)}, u32[]{:S(2)}) copy-start(f32[11,1024]{1,0:T(8,128)} %param.5) | copy-start | bytes 135172
  6.5 151.4 %all-reduce.8.cloned.1.call-start = ((), (), s32[]{:S(2)}) async-start(), calls=%async_computation.1 | async-start | bytes 12582912 | tf_op jit(solution)/shard_map/psum | solution.py:17
  16.9 403.4 %all-reduce.6.cloned.1.call-start = ((), (), s32[]{:S(2)}) async-start(), calls=%async_computation | async-start | bytes 25165824 | tf_op jit(solution)/shard_map/psum | solution.py:17
  158.0 4.0 copy-start.2
  158.0 4.0 copy-start.3
  166.0 8.5 %copy-start.5 = (bf16[2,1,512,1024]{3,2,1,0:T(8,128)(2,1)S(1)}, bf16[2,1,512,1024]{3,2,1,0:T(8,128)(2,1)}, u32[]{:S(2)}) copy-start(bf16[2,1,512,1024]{3,2,1,0:T(8,128)(2,1)} %get-tuple-element.15) | copy-start | bytes 6291460
  174.4 2.3 copy-start.4
  423.1 1.6 copy-start.8
  423.1 2.2 copy-start.9
  425.8 1.6 copy-start.6
  425.8 2.2 copy-start.7
  429.0 14.8 %copy-start.10 = (bf16[1,512,1024]{2,1,0:T(8,128)(2,1)S(1)}, bf16[1,512,1024]{2,1,0:T(8,128)(2,1)}, u32[]{:S(2)}) copy-start(bf16[1,512,1024]{2,1,0:T(8,128)(2,1)} %get-tuple-element.33) | copy-start | bytes 3145732
  429.0 14.8 %copy-start.11 = (bf16[1,512,1024]{2,1,0:T(8,128)(2,1)S(1)}, bf16[1,512,1024]{2,1,0:T(8,128)(2,1)}, u32[]{:S(2)}) copy-start(bf16[1,512,1024]{2,1,0:T(8,128)(2,1)} %get-tuple-element.34) | copy-start | bytes 3145732
  429.0 14.8 %copy-start.12 = (bf16[1,512,1024]{2,1,0:T(8,128)(2,1)S(1)}, bf16[1,512,1024]{2,1,0:T(8,128)(2,1)}, u32[]{:S(2)}) copy-start(bf16[1,512,1024]{2,1,0:T(8,128)(2,1)} %get-tuple-element.48) | copy-start | bytes 3145732
  443.8 25.3 %copy-start.13 = (bf16[1,512,1024]{2,1,0:T(8,128)(2,1)S(1)}, bf16[1,512,1024]{2,1,0:T(8,128)(2,1)}, u32[]{:S(2)}) copy-start(bf16[1,512,1024]{2,1,0:T(8,128)(2,1)} %get-tuple-element.29) | copy-start | bytes 3145732
  443.8 25.3 %copy-start.14 = (bf16[1,512,1024]{2,1,0:T(8,128)(2,1)S(1)}, bf16[1,512,1024]{2,1,0:T(8,128)(2,1)}, u32[]{:S(2)}) copy-start(bf16[1,512,1024]{2,1,0:T(8,128)(2,1)} %get-tuple-element.30) | copy-start | bytes 3145732
  561.3 6.4 %copy-start.1 = (f32[11,1024]{1,0:T(8,128)S(1)}, f32[11,1024]{1,0:T(8,128)}, u32[]{:S(2)}) copy-start(f32[11,1024]{1,0:T(8,128)} %param.5) | copy-start | bytes 135172
Sparse Core Ops, SparseCore 0:
  17.0 140.8 all-reduce.7
  165.6 254.6 all-reduce.5
where the time goes:
time: 575 us
  waiting for transfers between devices  381 us (66%)
  matrix products  69.4 us (12%)
  other arithmetic  54.4 us (9%)
  blocking collectives  40.9 us (7%)
  between operations  18.1 us (3%)
  local copies, waits for them, and re-layouts  10.8 us (2%)
    psum x2, waiting for transfers between devices, spread(): return lax.psum(block, axis)  381 us
    dot_general x3, matrix products, local(): jnp.einsum('yga,yah->ygh', left_factor, right_factor, preferred_element_t...  69 us
    psum x1, blocking collectives, local(): energy_data = lax.psum(local_data, ('row', 'col'))  40.9 us
    another operation x2, other arithmetic, local(): jnp.stack([wavefield[0].astype(jnp.float32) - sub_re, wavefield[1].astype...  18.6 us
    select_n x3, other arithmetic, spread(): jnp.where(lax.axis_index(axis) == holder, block, jnp.zeros_like(block))  14.5 us
  transfers between devices with their start and end apart: 2, of which 2 were waited for; matrix products, arithmetic and copies ran while one was open for 2% of the time, Pallas kernels for 0%

commit v1 on v0

--- a/solution.py
+++ b/solution.py
@@ -1,8 +1,10 @@
+import functools
 import math
 import jax
 import jax.numpy as jnp
 from jax import lax
 from jax.sharding import PartitionSpec as P
+from jax.lax import psum
 
 SIDE = 8192
 PANEL = 512
@@ -10,6 +12,13 @@
 TAPS = 11
 FIRST_FREQUENCY = 8
 NT = 1024
+
+
+def work_notes(slab_in, mesh_dim, lane_axis):
+    return psum(psum(slab_in, mesh_dim), lane_axis)
+
+
+place_table = functools.partial(work_notes, mesh_dim="col", lane_axis="row")
 
 
 def spread(block, axis, holder):
@@ -34,7 +43,7 @@
     factor = 1.0 / math.sqrt(STEPS * PANEL)
     count = 2.0 * SIDE * SIDE
     local_data = jnp.sum(jnp.square(wavefield.astype(jnp.float32)), axis=(0, 2, 3))
-    energy_data = lax.psum(local_data, ("row", "col"))
+    energy_data = place_table(local_data)
     totals = jnp.zeros((freq_count, shot_block, 2 * recv_block), jnp.float32)
     for panel_advance in range(STEPS):
         first_point = panel_order[panel_advance] * PANEL

time: 575 us -> 575 us (level)
  waiting for transfers between devices: 381 us -> 352 us
  blocking collectives: 40.9 us -> 68.4 us
    psum x2, waiting for transfers between devices: 381 us -> 352 us  [spread(): return lax.psum(block, axis)]
    psum x1 -> x3, blocking collectives: 40.9 us -> 68.4 us  [the longest x1 40.9 us: local(): energy_mult = lax.psum(local_mult, ('row', 'col'))]
  transfers between devices with their start and end apart: 2 -> 2, of which waited for: 2 -> 2; matrix products, arithmetic and copies ran while one was open for 2% -> 3% of each run, Pallas kernels for 0% -> 0%
where the time goes in v1:
time: 575 us; the launch traced here: 574 us
  waiting for transfers between devices  352 us (61%)
  matrix products  69.5 us (12%)
  blocking collectives  68.4 us (12%)
  other arithmetic  54.1 us (9%)
  between operations  18.5 us (3%)
  local copies, waits for them, and re-layouts  11.6 us (2%)
    psum x2, waiting for transfers between devices, spread(): return lax.psum(block, axis)  352 us
    dot_general x3, matrix products, local(): jnp.einsum('yga,yah->ygh', left_factor, right_factor, preferred_element_t...  69.1 us
    psum x1, blocking collectives, local(): energy_mult = lax.psum(local_mult, ('row', 'col'))  40.9 us
    psum x2, blocking collectives, work_notes(): return psum(psum(slab_in, mesh_dim), lane_axis)  27.5 us
    another operation x2, other arithmetic, local(): jnp.stack([wavefield[0].astype(jnp.float32) - sub_re, wavefield[1].astype...  18.6 us
    select_n x3, other arithmetic, spread(): jnp.where(lax.axis_index(axis) == holder, block, jnp.zeros_like(block))  14.4 us
  transfers between devices with their start and end apart: 2, of which 2 were waited for; matrix products, arithmetic and copies ran while one was open for 3% of the time, Pallas kernels for 0%

profile of v1, /device:TPU:0, one launch (start us, length us, event | category | flops | bytes accessed | tf_op | source)
XLA Modules:
  0.0 574.4 jit_solution(11574500970910910275)
XLA Ops:
  6.5 1.4 fusion.46
  10.0 7.0 %dynamic-slice_select_fusion = (bf16[2,1,512,1024]{3,2,1,0:T(8,128)(2,1)}, bf16[2,1,512,1024]{3,2,1,0:T(8,128)(2,1)}, bf16[2,1,512,1024]{3,2,1,0:T(8,128)(2,1)}) fusion(bf16[2,1,2048,1024]{3,2,1,0:T(8,128)(2,1)} %param.3, s32[]{:T(128)S(6)} %select_n.113, pred[]{:T(512)S(6)} %eq.27, s32[]{:T(128)S(6)} %select_n.106, pred[]{:T(512)S(6)} %eq.26, ...), kind=kLoop, calls=%fused_computation.52 | loop fusion | flops 3145728 | bytes 12582927 | tf_op jit(solution)/shard_map/jit(_where)/select_n | solution.py:25
  17.0 141.0 %all-reduce.7.cloned.1.call-done = (bf16[2,1,512,1024]{3,2,1,0:T(8,128)(2,1)}, bf16[2,1,512,1024]{3,2,1,0:T(8,128)(2,1)}, bf16[2,1,512,1024]{3,2,1,0:T(8,128)(2,1)}) async-done(((bf16[2,1,512,1024]{3,2,1,0:T(8,128)(2,1)}, bf16[2,1,512,1024]{3,2,1,0:T(8,128)(2,1)}, bf16[2,1,512,1024]{3,2,1,0:T(8,128)(2,1)}), (bf16[2,1,512,1024]{3,2,1,0:T(8,128)(2,1)}, bf16[2,1,512,1024]{3,2,1,0:T(8,128)(2,1)}, ...) | async-done | bytes 6291472 | tf_op jit(solution)/shard_map/psum | solution.py:26
  158.0 4.0 broadcast_select_fusion.5
  162.0 3.4 broadcast_select_fusion.3
  165.5 8.3 %multiply_reduce_fusion = f32[]{:T(128)} fusion(bf16[2,1,2048,1024]{3,2,1,0:T(8,128)(2,1)} %param.3), kind=kLoop, calls=%fused_computation.1 | loop fusion | flops 12582911 | bytes 8388612 | tf_op jit(solution)/shard_map/reduce_sum | solution.py:45
  173.8 17.7 %psum.84 = f32[1]{0:T(128)} all-reduce(f32[1]{0:T(128)} %bitcast.1), channel_id=1, replica_groups=mesh['row'=4,'col'=8] {'col'}, use_global_device_ids=true, to_apply=%region_1.0 | all-reduce | flops 1 | bytes 8 | tf_op jit(solution)/shard_map/psum | solution.py:18
  191.5 9.8 %psum.85 = f32[1]{0:T(128)} all-reduce(f32[1]{0:T(128)} %psum.84), channel_id=1, replica_groups=mesh['row'=4,'col'=8] {'row'}, use_global_device_ids=true, to_apply=%region_2.0 | all-reduce | flops 1 | bytes 8 | tf_op jit(solution)/shard_map/psum | solution.py:18
  202.1 0.2 fusion.30
  202.3 0.2 fusion.32
  202.6 0.1 fusion.45
  202.7 3.0 slice_bitcast_fusion.10
  205.7 1.5 fusion.43
  207.2 2.1 slice_bitcast_fusion.6
  209.3 211.3 %all-reduce.5.cloned.1.call-done = (bf16[2,1,512,1024]{3,2,1,0:T(8,128)(2,1)}, bf16[2,1,512,1024]{3,2,1,0:T(8,128)(2,1)}, bf16[2,1,512,1024]{3,2,1,0:T(8,128)(2,...) async-done(((bf16[2,1,512,1024]{3,2,1,0:T(8,128)(2,1)}, bf16[2,1,512,1024]{3,2,1,0:T(8,128)(2,1)}, ...) | async-done | bytes 12582928 | tf_op jit(solution)/shard_map/psum | solution.py:26
  420.6 2.7 maximum_bitcast_fusion
  423.4 0.3 slice_bitcast_fusion.5
  423.7 1.3 copy-done.8
  425.0 0.6 copy-done.9
  425.6 0.4 maximum_bitcast_fusion.5
  426.1 0.6 slice_bitcast_fusion.3
  426.6 1.0 copy-done.6
  427.6 0.6 copy-done.7
  428.3 0.4 maximum_bitcast_fusion.10
  428.7 0.6 slice_bitcast_fusion.1
  429.3 14.8 %fusion.13 = f32[2048,2048]{1,0:T(8,128)} fusion(bf16[1,2048,512]{1,2,0:T(8,128)(2,1)S(1)} %get-tuple-element.24, bf16[1,2048,512]{1,2,0:T(8,128)(2,1)S(1)} %get-tuple-element.23, bf16[1,512,1024]{2,1,0:T(8,128)(2,1)} %get-tuple-element.44, bf16[1,512,1024]{2,1,0:T(8,128)(2,1)} %get-tuple-element.47, bf16[1,512,1024]{2,1,0:T(8,128)(2,1)} %get-tuple-element.45), kind=kOutput, calls=%fused_computation.25 | convolution fusion | flops 8615100416 | bytes 24117248 | tf_op jit(solution)/shard_map/yga,yah->ygh/dot_general | solution.py:70
  444.1 25.4 %fusion.4 = f32[2048,2048]{1,0:T(8,128)} fusion(bf16[1,2048,512]{1,2,0:T(8,128)(2,1)S(1)} %get-tuple-element.26, bf16[1,2048,512]{1,2,0:T(8,128)(2,1)S(1)} %get-tuple-element.25, bf16[1,512,1024]{2,1,0:T(8,128)(2,1)S(1)} %copy-done.11, bf16[1,512,1024]{2,1,0:T(8,128)(2,1)S(1)} %copy-done.12, bf16[1,512,1024]{2,1,0:T(8,128)(2,1)S(1)} %copy-done.10), kind=kOutput, calls=%fused_computation.13 | convolution fusion | flops 8615100416 | bytes 24117248 | tf_op jit(solution)/shard_map/yga,yah->ygh/dot_general | solution.py:70
  469.5 28.9 %add_bitcast_fusion = f32[1,2048,2048]{2,1,0:T(8,128)} fusion(f32[2048,2048]{1,0:T(8,128)} %fusion.4, f32[2048,2048]{1,0:T(8,128)} %fusion.13, bf16[1,2048,512]{1,2,0:T(8,128)(2,1)S(1)} %get-tuple-element.22, bf16[1,2048,512]{1,2,0:T(8,128)(2,1)S(1)} %get-tuple-element.21, bf16[1,512,1024]{2,1,0:T(8,128)(2,1)S(1)} %copy-done.14, ...), kind=kOutput, calls=%fused_computation | convolution fusion | flops 8623489024 | bytes 57671680 | tf_op jit(solution)/shard_map/yga,yah->ygh/dot_general | solution.py:70
  498.4 7.6 %multiply_reduce_fusion.1 = (f32[]{:T(128)}, f32[]{:T(128)}) fusion(f32[1,2048,2048]{2,1,0:T(8,128)} %add_bitcast_fusion), kind=kLoop, calls=%fused_computation.7 | loop fusion | flops 12582910 | bytes 16777224 | tf_op jit(solution)/shard_map/reduce_sum | solution.py:75
  507.3 40.9 %psum.95 = f32[1]{0:T(128)} all-reduce(f32[1]{0:T(128)} %bitcast.27), channel_id=1, replica_groups=mesh['row'=4,'col'=8] {'row','col'}, use_global_device_ids=true, to_apply=%region_14.15 | all-reduce | flops 1 | bytes 8 | tf_op jit(solution)/shard_map/psum | solution.py:76
  548.9 12.3 %fusion.2 = (bf16[1,1,2048,1024]{3,2,1,0:T(8,128)(2,1)S(1)}, bf16[1,1,2048,1024]{3,2,1,0:T(8,128)(2,1)}) fusion(f32[1,2048,2048]{2,1,0:T(8,128)} %add_bitcast_fusion, f32[1024]{0:T(1024)S(1)} %get-tuple-element.48, f32[1024]{0:T(1024)S(1)} %get-tuple-element.49, f32[]{:T(128)} %bitcast.28, bf16[2,1,2048,1024]{3,2,1,0:T(8,128)(2,1)} %param.3), kind=kLoop, calls=%fused_computation.9 | loop fusion | flops 29360128 | bytes 33562628 | tf_op jit(solution)/shard_map/stack | solution.py:83
  561.1 6.4 %pad_maximum_fusion = bf16[2,1,2048,1024]{3,2,1,0:T(8,128)(2,1)} fusion(bf16[1,1,2048,1024]{3,2,1,0:T(8,128)(2,1)} %get-tuple-element.17, bf16[1,1,2048,1024]{3,2,1,0:T(8,128)(2,1)S(1)} %get-tuple-element.16), kind=kLoop, calls=%fused_computation.2 | loop fusion | flops 4194304 | bytes 16777216 | tf_op jit(solution)/shard_map/stack | solution.py:83
  (31 shorter events, 0.1 us)
Async XLA Ops:
  6.5 195.6 %copy-start = (f32[11,1024]{1,0:T(8,128)S(1)}, f32[11,1024]{1,0:T(8,128)}, u32[]{:S(2)}) copy-start(f32[11,1024]{1,0:T(8,128)} %param.5) | copy-start | bytes 135172
  6.5 151.5 %all-reduce.7.cloned.1.call-start = ((), (), s32[]{:S(2)}) async-start(), calls=%async_computation.1 | async-start | bytes 12582912 | tf_op jit(solution)/shard_map/psum | solution.py:26
  16.9 403.7 %all-reduce.5.cloned.1.call-start = ((), (), s32[]{:S(2)}) async-start(), calls=%async_computation | async-start | bytes 25165824 | tf_op jit(solution)/shard_map/psum | solution.py:26
  158.0 4.0 copy-start.2
  158.0 4.1 copy-start.3
  201.3 4.4 copy-start.4
  201.3 4.4 copy-start.5
  423.4 1.6 copy-start.8
  423.4 2.2 copy-start.9
  426.0 1.6 copy-start.6
  426.0 2.2 copy-start.7
  429.3 14.8 %copy-start.10 = (bf16[1,512,1024]{2,1,0:T(8,128)(2,1)S(1)}, bf16[1,512,1024]{2,1,0:T(8,128)(2,1)}, u32[]{:S(2)}) copy-start(bf16[1,512,1024]{2,1,0:T(8,128)(2,1)} %get-tuple-element.31) | copy-start | bytes 3145732
  429.3 14.8 %copy-start.11 = (bf16[1,512,1024]{2,1,0:T(8,128)(2,1)S(1)}, bf16[1,512,1024]{2,1,0:T(8,128)(2,1)}, u32[]{:S(2)}) copy-start(bf16[1,512,1024]{2,1,0:T(8,128)(2,1)} %get-tuple-element.32) | copy-start | bytes 3145732
  429.3 14.8 %copy-start.12 = (bf16[1,512,1024]{2,1,0:T(8,128)(2,1)S(1)}, bf16[1,512,1024]{2,1,0:T(8,128)(2,1)}, u32[]{:S(2)}) copy-start(bf16[1,512,1024]{2,1,0:T(8,128)(2,1)} %get-tuple-element.46) | copy-start | bytes 3145732
  444.1 25.4 %copy-start.13 = (bf16[1,512,1024]{2,1,0:T(8,128)(2,1)S(1)}, bf16[1,512,1024]{2,1,0:T(8,128)(2,1)}, u32[]{:S(2)}) copy-start(bf16[1,512,1024]{2,1,0:T(8,128)(2,1)} %get-tuple-element.27) | copy-start | bytes 3145732
  444.1 25.4 %copy-start.14 = (bf16[1,512,1024]{2,1,0:T(8,128)(2,1)S(1)}, bf16[1,512,1024]{2,1,0:T(8,128)(2,1)}, u32[]{:S(2)}) copy-start(bf16[1,512,1024]{2,1,0:T(8,128)(2,1)} %get-tuple-element.28) | copy-start | bytes 3145732
  561.1 6.4 %copy-start.1 = (f32[11,1024]{1,0:T(8,128)S(1)}, f32[11,1024]{1,0:T(8,128)}, u32[]{:S(2)}) copy-start(f32[11,1024]{1,0:T(8,128)} %param.5) | copy-start | bytes 135172
Sparse Core Ops, SparseCore 0:
  17.1 140.8 all-reduce.6
  165.6 254.9 all-reduce.4
